TPU v7x, 128 devices: a whole 4x4x4 slice. The times are simulated.
128 devices in a mesh: dp: 4 (over z_lo, core), mp: 32 (over y, z_hi, x).
Axes of the slice: x: 4, y: 4, z: 4 (z_hi: 2, z_lo: 2; z = z_hi * 2 + z_lo), core: 2. Of those that a mesh axis runs over, the one named last changes fastest.
Arguments:
- fields: float32 [4, 32, 128, 128, 128], P('dp', None, 'mp'), may hold values from -6 to 6
- upstream: bfloat16 [4, 32, 128, 128, 128], P('dp', None, 'mp'), may hold values from -6 to 6
- spectral_weight: float32 [2, 32, 32, 32, 1024], P(None, None, None, 'dp', 'mp'), may hold values from -4.2 to 4.2
- point_weight: float32 [32, 32], replicated, may hold values from -1 to 1
- point_bias: float32 [32], replicated, may hold values from -3 to 3
Outputs:
- grad_fields: float32 [4, 32, 128, 128, 128], P('dp', None, 'mp')
- grad_weight: float32 [2, 32, 32, 32, 1024], P(None, None, None, 'dp', 'mp')
All inputs are finite; a program needn't handle non-finite values.
Results may differ from a plain program's by a relative error of at most 0.0003.
Values sent between devices are 32-bit elements; how exact they have to be, the bound alone decides.
A program may use at most 256 MiB of HBM per device.

v0:
```python
from functools import partial
import math
import jax
import jax.numpy as jnp
from jax import lax
from jax.sharding import PartitionSpec as P

NX = 128
NY = 128
NZ = 128
MX = 32
MY = 32
MZ = 32
HIGHEST = lax.Precision.HIGHEST


def tables(number, kept_modes, signed):
    positions = jnp.arange(number, dtype=jnp.int32)
    frequency = jnp.arange(kept_modes, dtype=jnp.int32)
    if signed:
        frequency = jnp.where(frequency < kept_modes // 2, frequency, frequency - kept_modes)
    phases = jnp.mod(positions[:, None] * frequency[None, :], number).astype(jnp.float32) * (
        2.0 * math.pi / number
    )
    return jnp.concatenate([jnp.cos(phases), jnp.sin(phases)], axis=1)


def forward_plane(grid_field, table_y, table_z):
    along_y = jnp.einsum("scpyz,yj->scpjz", grid_field, table_y, precision=HIGHEST)
    products = jnp.einsum("scpjz,zk->scpjk", along_y, table_z, precision=HIGHEST)
    cos_cos = products[:, :, :, :MY, :MZ]
    cos_sin = products[:, :, :, :MY, MZ:]
    sin_cos = products[:, :, :, MY:, :MZ]
    sin_sin = products[:, :, :, MY:, MZ:]
    result = jnp.stack([cos_cos - sin_sin, -(sin_cos + cos_sin)], axis=3)
    return result.reshape(result.shape[:4] + (MY * MZ,))


def forward_line(pieces, table_x):
    products = jnp.einsum("scxrm,xk->scrkm", pieces, table_x, precision=HIGHEST)
    real_part = products[:, :, 0, :MX] + products[:, :, 1, MX:]
    imag_part = products[:, :, 1, :MX] - products[:, :, 0, MX:]
    return jnp.stack([real_part, imag_part], axis=2)


def inverse_line(spectrum, table_x):
    real_part = spectrum[:, :, 0]
    imag_part = spectrum[:, :, 1]
    stacked = jnp.stack(
        [
            jnp.concatenate([real_part, -imag_part], axis=2),
            jnp.concatenate([imag_part, real_part], axis=2),
        ],
        axis=2,
    )
    return jnp.einsum("scrjm,xj->scxrm", stacked, table_x, precision=HIGHEST)


def inverse_plane(pieces, table_y, table_z):
    shaped = pieces.reshape(pieces.shape[:4] + (MY, MZ))
    real_part = shaped[:, :, :, 0]
    imag_part = shaped[:, :, :, 1]
    stacked = jnp.stack(
        [
            jnp.concatenate([real_part, -imag_part], axis=3),
            jnp.concatenate([imag_part, real_part], axis=3),
        ],
        axis=3,
    )
    along_y = jnp.einsum("scpwjk,yj->scpwyk", stacked, table_y, precision=HIGHEST)
    merged = jnp.concatenate([along_y[:, :, :, 0], -along_y[:, :, :, 1]], axis=4)
    return jnp.einsum("scpyj,zj->scpyz", merged, table_z, precision=HIGHEST)


def mix_forward(weight, spectrum):
    real_weight = weight[0]
    imag_weight = weight[1]
    real_spec = spectrum[:, :, 0]
    imag_spec = spectrum[:, :, 1]
    real_part = jnp.einsum(
        "sixm,ioxm->soxm", real_spec, real_weight, precision=HIGHEST
    ) - jnp.einsum("sixm,ioxm->soxm", imag_spec, imag_weight, precision=HIGHEST)
    imag_part = jnp.einsum(
        "sixm,ioxm->soxm", imag_spec, real_weight, precision=HIGHEST
    ) + jnp.einsum("sixm,ioxm->soxm", real_spec, imag_weight, precision=HIGHEST)
    return jnp.stack([real_part, imag_part], axis=2)


def mix_adjoint(weight, gradient):
    real_weight = weight[0]
    imag_weight = weight[1]
    real_grad = gradient[:, :, 0]
    imag_grad = gradient[:, :, 1]
    real_part = jnp.einsum(
        "soxm,ioxm->sixm", real_grad, real_weight, precision=HIGHEST
    ) + jnp.einsum("soxm,ioxm->sixm", imag_grad, imag_weight, precision=HIGHEST)
    imag_part = jnp.einsum(
        "soxm,ioxm->sixm", imag_grad, real_weight, precision=HIGHEST
    ) - jnp.einsum("soxm,ioxm->sixm", real_grad, imag_weight, precision=HIGHEST)
    return jnp.stack([real_part, imag_part], axis=2)


def weight_gradient(gradient, spectrum):
    real_grad = gradient[:, :, 0]
    imag_grad = gradient[:, :, 1]
    real_spec = spectrum[:, :, 0]
    imag_spec = spectrum[:, :, 1]
    real_part = jnp.einsum("soxm,sixm->ioxm", real_grad, real_spec, precision=HIGHEST) + jnp.einsum(
        "soxm,sixm->ioxm", imag_grad, imag_spec, precision=HIGHEST
    )
    imag_part = jnp.einsum("soxm,sixm->ioxm", imag_grad, real_spec, precision=HIGHEST) - jnp.einsum(
        "soxm,sixm->ioxm", real_grad, imag_spec, precision=HIGHEST
    )
    return jnp.stack([real_part, imag_part], axis=0)


def shards(fields, upstream, spectral_weight, point_weight, point_bias):
    table_y = tables(NY, MY, True)
    table_z = tables(NZ, MZ, False)
    table_x = tables(NX, MX, True)
    modes_dev = spectral_weight.shape[4]
    mode_index = lax.axis_index("mp") * modes_dev + jnp.arange(modes_dev, dtype=jnp.int32)
    kz_index = jnp.mod(mode_index, MZ)
    factor = jnp.where(kz_index == 0, 1.0, 2.0).astype(jnp.float32) / float(NX * NY * NZ)

    def to_modes(pieces):
        return forward_line(pieces, table_x)

    def to_cells(pieces):
        return inverse_plane(pieces, table_y, table_z)

    spectrum = to_modes(
        lax.all_to_all(
            forward_plane(fields, table_y, table_z), "mp", split_axis=4, concat_axis=2, tiled=True
        )
    )
    full_weight = lax.all_gather(spectral_weight, "dp", axis=3, tiled=True)
    mixed_spec = mix_forward(full_weight, spectrum)
    mixed_spec = mixed_spec * factor
    spectral_part = to_cells(
        lax.all_to_all(
            inverse_line(mixed_spec, table_x), "mp", split_axis=2, concat_axis=4, tiled=True
        )
    )
    preact = spectral_part + jnp.einsum("scpyz,co->sopyz", fields, point_weight, precision=HIGHEST)
    preact = preact + point_bias[None, :, None, None, None]
    activation, pullback = jax.vjp(partial(jax.nn.gelu, approximate=False), preact)
    grad_pre = pullback(upstream.astype(jnp.float32))[0]
    grad_spec = to_modes(
        lax.all_to_all(
            forward_plane(grad_pre, table_y, table_z), "mp", split_axis=4, concat_axis=2, tiled=True
        )
    )
    grad_spec = grad_spec * factor
    back_spec = mix_adjoint(full_weight, grad_spec)
    weight_out = lax.psum_scatter(
        weight_gradient(grad_spec, spectrum), "dp", scatter_dimension=3, tiled=True
    )
    spectral_back = to_cells(
        lax.all_to_all(
            inverse_line(back_spec, table_x), "mp", split_axis=2, concat_axis=4, tiled=True
        )
    )
    grad_fields = spectral_back + jnp.einsum(
        "sopyz,co->scpyz", grad_pre, point_weight, precision=HIGHEST
    )
    return (grad_fields, weight_out)


def solution(mesh):
    placed = (
        P("dp", None, "mp", None, None),
        P("dp", None, "mp", None, None),
        P(None, None, None, "dp", "mp"),
        P(),
        P(),
    )
    return jax.shard_map(
        shards,
        mesh=mesh,
        in_specs=placed,
        out_specs=(P("dp", None, "mp", None, None), P(None, None, None, "dp", "mp")),
        check_vma=False,
    )
```

profile of v0, /device:TPU:1, one launch (start us, length us, event | category | flops | bytes accessed | tf_op | source)
XLA Modules:
  0.0 849.2 jit_solution(7774384556777394916)
XLA Ops:
  8.2 6.8 fusion.70
  15.0 3.6 fusion.46
  21.1 3.6 copy.236
  27.2 9.9 %fusion.108 = f32[1024,1,4,2,32]{4,3,2,1,0:T(2,128)} fusion(f32[1,32,4,1,1024]{1,3,2,0,4:T(1,128)} %bitcast.341, f32[1,32,4,1,1024]{1,3,2,0,4:T(1,128)} %bitcast.339), kind=kLoop, calls=%fused_computation.186 | loop fusion | flops 262144 | bytes 2097152
  37.1 6.7 reshape.415
  43.8 11.3 %all-to-all-start = ((f32[32,1,8192]{2,1,0:T(1,128)}), f32[32,1,8192]{2,1,0:T(1,128)S(1)}, u32[]{:S(2)}, u32[]{:S(2)}) async-start(f32[32,1,8192]{2,1,0:T(1,128)} %reshape.415), calls=%async_computation | async-start | bytes 2097152 | tf_op jit(solution)/shard_map/all_to_all | solution.py:133
  55.2 17.2 %all-to-all-done = f32[32,1,8192]{2,1,0:T(1,128)S(1)} async-done(((f32[32,1,8192]{2,1,0:T(1,128)}), f32[32,1,8192]{2,1,0:T(1,128)S(1)}, u32[]{:S(2)}, u32[]{:S(2)}) %all-to-all-start) | async-done | bytes 1048608 | tf_op jit(solution)/shard_map/all_to_all | solution.py:133
  72.9 3.3 reduce.16
  76.2 4.9 reshape.416
  81.0 7.4 copy.238
  88.4 6.6 copy.146
  95.1 3.8 copy.147
  100.5 214.9 %all-gather.2.cloned.1.call-done = f32[2,32,32,32,32]{4,3,2,1,0:T(8,128)} async-done(((f32[2,32,32,8,32]{4,3,2,1,0:T(8,128)}), f32[2,32,32,32,32]{4,3,2,1,0:T(8,128)}) %all-gather.2.cloned.1.call-update) | async-done | bytes 8388624 | tf_op jit(solution)/shard_map/all_gather | solution.py:137
  315.5 13.5 %fusion.4 = (f32[32,32,32]{1,0,2:T(8,128)S(1)}, f32[32,32,32]{1,0,2:T(8,128)S(1)}, f32[32,32,32]{1,0,2:T(8,128)S(1)}, f32[32,32,32]{1,0,2:T(8,128)S(1)}) fusion(f32[2,32,32,32,32]{4,3,2,1,0:T(8,128)} %all-gather.2.cloned.1.call-done, f32[32,32,32]{1,0,2:T(8,128)S(1)} %copy.250, f32[32,32,32]{1,0,2:T(8,128)S(1)} %copy.249), kind=kLoop, calls=%fused_computation.11 | loop fusion | flops 8257536 | bytes 9175040
  333.5 4.3 copy.149
  337.8 6.5 reshape.417
  344.3 9.1 %all-to-all-start.1 = ((f32[32,1,8192]{2,1,0:T(1,128)}), f32[32,1,8192]{2,1,0:T(1,128)S(1)}, u32[]{:S(2)}, u32[]{:S(2)}) async-start(f32[32,1,8192]{2,1,0:T(1,128)} %reshape.417), calls=%async_computation.1 | async-start | bytes 2097152 | tf_op jit(solution)/shard_map/all_to_all | solution.py:141
  353.5 16.3 %fusion.21 = f32[32,4,128,128]{3,0,2,1:T(8,128)} fusion(f32[32,4,128,128]{3,2,1,0:T(8,128)} %bitcast.318, f32[32,32]{1,0:T(8,128)S(1)} %copy-done), kind=kOutput, calls=%fused_computation.37 | convolution fusion | flops 805306368 | bytes 16781312 | tf_op jit(solution)/shard_map/scpyz,co->sopyz/dot_general | solution.py:145
  371.3 3.3 reduce.17
  374.6 4.9 reshape.418
  379.5 7.9 copy.151
  393.1 3.4 fusion.53
  397.7 44.8 %fusion.13 = f32[32,4,128,128]{3,2,1,0:T(8,128)S(1)} fusion(bf16[1,32,4,128,128]{4,3,2,1,0:T(8,128)(2,1)S(1)} %copy-done.2, f32[32,4,128,128]{3,0,2,1:T(8,128)S(1)} %bitcast.338, f32[32]{0:T(128)S(1)} %copy-done.3, f32[1,32,4,128,32]{3,4,2,1,0:T(8,128)S(1)} %get-tuple-element.23, f32[1,32,4,128,32]{3,4,2,1,0:T(8,128)S(1)} %get-tuple-element.22, ...), kind=kOutput, calls=%fused_computation.27 | convolution fusion | flops 1766858752 | bytes 25198720 | tf_op jit(solution)/shard_map/scpyj,zj->scpyz/dot_general | solution.py:72
  442.6 3.4 copy-done.1
  446.0 5.3 fusion.67
  451.3 3.6 fusion.49
  457.4 3.4 copy.242
  463.3 8.9 %fusion.107 = f32[1024,1,4,2,32]{4,3,2,1,0:T(2,128)} fusion(f32[1,32,4,1,1024]{1,3,2,0,4:T(1,128)} %bitcast.342, f32[1,32,4,1,1024]{1,3,2,0,4:T(1,128)} %bitcast.340), kind=kLoop, calls=%fused_computation.185 | loop fusion | flops 262144 | bytes 2097152
  472.2 5.8 reshape.419
  478.0 26.0 %all_to_all.60 = f32[32,1,8192]{2,1,0:T(1,128)S(1)} all-to-all(f32[32,1,8192]{2,1,0:T(1,128)S(1)} %reshape.419), channel_id=1, replica_groups=mesh['dp'=4,'mp'=32] {'mp'}, dimensions={0} | all-to-all | bytes 2097152 | tf_op jit(solution)/shard_map/all_to_all | solution.py:150
  503.9 3.3 reduce.18
  507.2 4.9 reshape.420
  512.1 7.5 copy.244
  519.6 6.6 copy.160
  526.2 3.8 copy.161
  532.1 5.8 add_bitcast_fusion
  537.9 14.0 %pad_maximum_fusion = f32[2,32,32,32,32]{4,3,2,1,0:T(8,128)} fusion(f32[1,32,32,32,32]{4,3,2,1,0:T(8,128)S(1)} %get-tuple-element.29, f32[1,32,32,32,32]{4,3,2,1,0:T(8,128)S(1)} %get-tuple-element.28), kind=kLoop, calls=%fused_computation | loop fusion | flops 2097152 | bytes 16777216 | tf_op jit(solution)/shard_map/stack | solution.py:114
  552.0 15.6 %fusion.1 = (f32[32,32,32]{1,0,2:T(8,128)S(1)}, f32[32,32,32]{1,0,2:T(8,128)S(1)}, f32[32,32,32]{1,0,2:T(8,128)S(1)}, f32[32,32,32]{1,0,2:T(8,128)S(1)}) fusion(f32[2,32,32,32,32]{4,3,2,1,0:T(8,128)} %all-gather.2.cloned.1.call-done, f32[32,32,32]{1,0,2:T(8,128)S(1)} %copy.251, f32[32,32,32]{1,0,2:T(8,128)S(1)} %copy.252), kind=kLoop, calls=%fused_computation.4 | loop fusion | flops 8257536 | bytes 9175040
  571.7 4.5 copy.164
  576.3 6.5 reshape.421
  582.8 5.6 all-to-all-start.3
  588.4 17.7 %fusion.18 = f32[4,128,128,32]{2,3,1,0:T(8,128)} fusion(f32[32,4,128,128]{3,2,1,0:T(8,128)} %copy-done.1, f32[32,32]{1,0:T(8,128)S(1)} %copy-done), kind=kOutput, calls=%fused_computation.33 | convolution fusion | flops 805306368 | bytes 16781312 | tf_op jit(solution)/shard_map/sopyz,co->scpyz/dot_general | solution.py:164
  606.1 3.3 reduce.19
  609.4 4.9 reshape.422
  614.3 7.8 copy.166
  627.8 3.4 fusion.52
  631.8 22.5 %fusion.17 = f32[1,32,4,128,128]{4,3,2,1,0:T(8,128)} fusion(f32[4,128,128,32]{2,3,1,0:T(8,128)S(1)} %bitcast.320, f32[1,32,4,128,32]{3,4,2,1,0:T(8,128)S(1)} %get-tuple-element.17, f32[1,32,4,128,32]{3,4,2,1,0:T(8,128)S(1)} %get-tuple-element.16, f32[128,32]{0,1:T(8,128)S(1)} %get-tuple-element.48, f32[128,32]{0,1:T(8,128)S(1)} %get-tuple-element.49), kind=kOutput, calls=%fused_computation.32 | convolution fusion | flops 1613766656 | bytes 21004288 | tf_op jit(solution)/shard_map/scpyj,zj->scpyz/dot_general | solution.py:72
  654.3 187.8 %reduce-scatter.2.cloned.1.call-done = f32[2,32,32,8,32]{4,3,2,1,0:T(8,128)} async-done(((f32[2,32,32,32,32]{4,3,2,1,0:T(8,128)}), f32[2,32,32,8,32]{4,3,2,1,0:T(8,128)}) %reduce-scatter.2.cloned.1.call-update) | async-done | bytes 2097168 | tf_op jit(solution)/shard_map/reduce_scatter | solution.py:156
  (70 shorter events, 38.4 us)
Async XLA Ops:
  7.2 346.3 %copy-start = (f32[32,32]{1,0:T(8,128)S(1)}, f32[32,32]{1,0:T(8,128)}, u32[]{:S(2)}) copy-start(f32[32,32]{1,0:T(8,128)} %param.8) | copy-start | bytes 12292
  7.2 308.3 %all-gather.2.cloned.1.call-start = ((), (), s32[]{:S(2)}) async-start(), calls=%async_computation.5 | async-start | bytes 41943040 | tf_op jit(solution)/shard_map/all_gather | solution.py:137
  43.8 28.5 %all-to-all-start = ((f32[32,1,8192]{2,1,0:T(1,128)}), f32[32,1,8192]{2,1,0:T(1,128)S(1)}, u32[]{:S(2)}, u32[]{:S(2)}) async-start(f32[32,1,8192]{2,1,0:T(1,128)} %reshape.415), calls=%async_computation | async-start | bytes 2097152 | tf_op jit(solution)/shard_map/all_to_all | solution.py:133
  344.3 27.0 %all-to-all-start.1 = ((f32[32,1,8192]{2,1,0:T(1,128)}), f32[32,1,8192]{2,1,0:T(1,128)S(1)}, u32[]{:S(2)}, u32[]{:S(2)}) async-start(f32[32,1,8192]{2,1,0:T(1,128)} %reshape.417), calls=%async_computation.1 | async-start | bytes 2097152 | tf_op jit(solution)/shard_map/all_to_all | solution.py:141
  353.4 488.6 %reduce-scatter.2.cloned.1.call-start = ((), (), s32[]{:S(2)}) async-start(), calls=%async_computation.6 | async-start | bytes 41943040 | tf_op jit(solution)/shard_map/reduce_scatter | solution.py:156
  393.1 4.2 slice-start.2
  393.1 4.2 slice-start.3
  393.1 4.6 copy-start.2
  393.1 4.6 copy-start.3
  442.6 3.4 copy-start.1
  582.8 23.4 %all-to-all-start.3 = ((f32[32,1,8192]{2,1,0:T(1,128)}), f32[32,1,8192]{2,1,0:T(1,128)S(1)}, u32[]{:S(2)}, u32[]{:S(2)}) async-start(f32[32,1,8192]{2,1,0:T(1,128)} %reshape.421), calls=%async_computation.3 | async-start | bytes 2097152 | tf_op jit(solution)/shard_map/all_to_all | solution.py:160
  627.8 3.9 slice-start
  627.8 3.9 slice-start.1
Sparse Core Ops, SparseCore 0:
  9.7 305.7 all-gather.1
  552.1 289.8 reduce-scatter.1
where the time goes:
time: 857 us; the launch traced here: 849 us
  waiting for transfers between devices  422 us (49%)
  local copies, waits for them, and re-layouts  131 us (15%)
  matrix products  131 us (15%)
  other arithmetic  97.4 us (11%)
  starting transfers between devices  26.2 us (3%)
  blocking collectives  26 us (3%)
  between operations  15 us (2%)
    all_gather x1, waiting for transfers between devices, shards(): full_weight = lax.all_gather(spectral_weight, 'dp', axis=3, tiled=True)  215 us
    reduce_scatter x1, waiting for transfers between devices, shards(): lax.psum_scatter(weight_gradient(grad_spec, spectrum), 'dp', scatter_dime...  188 us
    dot_general x2, matrix products, inverse_plane(): return jnp.einsum('scpyj,zj->scpyz', merged, table_z, precision=HIGHEST)  67.3 us
    unnamed x29, local copies, waits for them, and re-layouts  49.8 us
    unnamed x7, other arithmetic  48.2 us
    all_to_all x1, blocking collectives, shards(): lax.all_to_all(forward_plane(grad_pre, table_y, table_z), 'mp', split_axi...  26 us
    another operation x2, other arithmetic, weight_gradient(): return jnp.stack([real_part, imag_part], axis=0)  19.8 us
    dot_general x1, matrix products, shards(): jnp.einsum('sopyz,co->scpyz', grad_pre, point_weight, precision=HIGHEST)  17.7 us
  transfers between devices with their start and end apart: 5, of which 4 were waited for; matrix products, arithmetic and copies ran while one was open for 21% of the time, Pallas kernels for 0%

commit v1 on v0

--- a/solution.py
+++ b/solution.py
@@ -134,7 +134,9 @@
             forward_plane(fields, table_y, table_z), "mp", split_axis=4, concat_axis=2, tiled=True
         )
     )
-    full_weight = lax.all_gather(spectral_weight, "dp", axis=3, tiled=True)
+    full_weight = jnp.concatenate(
+        lax.all_to_all(jnp.stack([spectral_weight] * lax.axis_size("dp")), "dp", 0, 0), axis=3
+    )
     mixed_spec = mix_forward(full_weight, spectrum)
     mixed_spec = mixed_spec * factor
     spectral_part = to_cells(

time: 857 us -> 820 us (0.957)
  waiting for transfers between devices: 422 us -> 254 us
  local copies, waits for them, and re-layouts: 131 us -> 232 us
  other arithmetic: 97.4 us -> 125 us
    all_gather x1 -> x0, waiting for transfers between devices: 215 us -> none  [shards(): full_weight = lax.all_gather(spectral_weight, 'dp', axis=3, tiled=True)]
    unnamed x29 -> x31, local copies, waits for them, and re-layouts: 49.8 us -> 114 us
    all_to_all x0 -> x1, waiting for transfers between devices: none -> 64.2 us  [shards(): lax.all_to_all(jnp.stack([spectral_weight] * lax.axis_size('dp')), 'dp',...]
    all_to_all x0 -> x1, other arithmetic: none -> 28.5 us  [shards(): lax.all_to_all(jnp.stack([spectral_weight] * lax.axis_size('dp')), 'dp',...]
    all_to_all x0 -> x2, local copies, waits for them, and re-layouts: none -> 23.8 us  [shards(): lax.all_to_all(jnp.stack([spectral_weight] * lax.axis_size('dp')), 'dp',...]
    all_to_all x1, waiting for transfers between devices: 17.2 us -> 0.01 us  [shards(): lax.all_to_all(forward_plane(fields, table_y, table_z), 'mp', split_axis=...]
    another operation x2 -> x3, local copies, waits for them, and re-layouts: 7.51 us -> 21.5 us  [the longest x1 13.9 us: shards(): jnp.stack([spectral_weight] * lax.axis_size('dp'))]
  transfers between devices with their start and end apart: 5 -> 5, of which waited for: 4 -> 3; matrix products, arithmetic and copies ran while one was open for 21% -> 23% of each run, Pallas kernels for 0% -> 0%
where the time goes in v1:
time: 820 us; the launch traced here: 812 us
  waiting for transfers between devices  254 us (31%)
  local copies, waits for them, and re-layouts  232 us (28%)
  matrix products  128 us (16%)
  other arithmetic  125 us (15%)
  starting transfers between devices  33 us (4%)
  blocking collectives  25.2 us (3%)
  between operations  15 us (2%)
    reduce_scatter x1, waiting for transfers between devices, shards(): lax.psum_scatter(weight_gradient(grad_spec, spectrum), 'dp', scatter_dime...  190 us
    unnamed x31, local copies, waits for them, and re-layouts  114 us
    all_to_all x1, waiting for transfers between devices, shards(): lax.all_to_all(jnp.stack([spectral_weight] * lax.axis_size('dp')), 'dp',...  64.2 us
    dot_general x2, matrix products, inverse_plane(): return jnp.einsum('scpyj,zj->scpyz', merged, table_z, precision=HIGHEST)  63.7 us
    unnamed x7, other arithmetic  47.3 us
    all_to_all x1, other arithmetic, shards(): lax.all_to_all(jnp.stack([spectral_weight] * lax.axis_size('dp')), 'dp',...  28.5 us
    all_to_all x1, blocking collectives, shards(): lax.all_to_all(forward_plane(grad_pre, table_y, table_z), 'mp', split_axi...  25.2 us
    all_to_all x2, local copies, waits for them, and re-layouts, shards(): lax.all_to_all(jnp.stack([spectral_weight] * lax.axis_size('dp')), 'dp',...  23.8 us
  transfers between devices with their start and end apart: 5, of which 3 were waited for; matrix products, arithmetic and copies ran while one was open for 23% of the time, Pallas kernels for 0%

profile of v1, /device:TPU:1, one launch (start us, length us, event | category | flops | bytes accessed | tf_op | source)
XLA Modules:
  0.0 812.1 jit_solution(4878672367859265267)
XLA Ops:
  7.4 6.8 fusion.70
  14.2 3.6 fusion.46
  26.2 8.9 %fusion.108 = f32[1024,1,4,2,32]{4,3,2,1,0:T(2,128)} fusion(f32[1,32,4,1,1024]{1,3,2,0,4:T(1,128)} %bitcast.344, f32[1,32,4,1,1024]{1,3,2,0,4:T(1,128)} %bitcast.346), kind=kLoop, calls=%fused_computation.187 | loop fusion | flops 262144 | bytes 2097152
  35.1 6.5 reshape.428
  41.6 11.2 %all-to-all-start = ((f32[32,1,8192]{2,1,0:T(1,128)}), f32[32,1,8192]{2,1,0:T(1,128)S(1)}, u32[]{:S(2)}, u32[]{:S(2)}) async-start(f32[32,1,8192]{2,1,0:T(1,128)} %reshape.428), calls=%async_computation | async-start | bytes 2097152 | tf_op jit(solution)/shard_map/all_to_all | solution.py:133
  52.8 13.9 %stack.87 = f32[4,2,32,32,8,32]{5,4,3,2,1,0:T(8,128)} broadcast(f32[2,32,32,8,32]{4,3,2,1,0:T(8,128)} %param.7), dimensions={1,2,3,4,5} | broadcast | bytes 10485760 | tf_op jit(solution)/shard_map/stack | solution.py:138
  66.7 33.4 %reshape.426 = f32[4,1,524288]{2,1,0:T(1,128)} reshape(f32[4,2,32,32,8,32]{5,4,3,2,1,0:T(8,128)} %stack.87) | data formatting | bytes 16777216
  100.2 7.0 all-to-all-start.1
  110.9 4.9 reshape.429
  115.8 7.5 copy.241
  123.2 6.6 copy.148
  129.9 3.8 copy.149
  135.4 64.2 %all-to-all-done.1 = f32[4,1,524288]{2,1,0:T(1,128)} async-done(((f32[4,1,524288]{2,1,0:T(1,128)}), f32[4,1,524288]{2,1,0:T(1,128)}, u32[]{:S(2)}, u32[]{:S(2)}) %all-to-all-start.1) | async-done | bytes 8388640 | tf_op jit(solution)/shard_map/all_to_all | solution.py:138
  199.5 28.5 %reduce.16 = f32[4,524288]{1,0:T(4,128)} reduce(f32[4,1,524288]{2,1,0:T(1,128)} %all-to-all-done.1, f32[]{:T(128)} %broadcast.198), dimensions={1}, to_apply=%all_to_all.50.reduce_sub_computation | reduce | bytes 16777220 | tf_op jit(solution)/shard_map/all_to_all | solution.py:138
  228.1 31.1 %reshape.427 = f32[4,2,32,32,8,32]{5,4,3,2,1,0:T(8,128)} reshape(f32[4,524288]{1,0:T(4,128)} %reduce.16) | data formatting | bytes 16777216
  259.1 23.3 %copy.268 = f32[4,2,32,32,8,32]{5,4,0,3,2,1:T(8,128)} copy(f32[4,2,32,32,8,32]{5,4,3,2,1,0:T(8,128)} %reshape.427) | data formatting | bytes 16777216 | tf_op jit(solution)/shard_map/all_to_all | solution.py:138
  282.4 13.4 %fusion.4 = (f32[32,32,32]{1,0,2:T(8,128)S(1)}, f32[32,32,32]{1,0,2:T(8,128)S(1)}, f32[32,32,32]{1,0,2:T(8,128)S(1)}, f32[32,32,32]{1,0,2:T(8,128)S(1)}) fusion(f32[2,32,32,4,8,32]{5,4,3,2,1,0:T(8,128)} %bitcast.321, f32[32,32,32]{1,0,2:T(8,128)S(1)} %copy.253, f32[32,32,32]{1,0,2:T(8,128)S(1)} %copy.252), kind=kLoop, calls=%fused_computation.12 | loop fusion | flops 8257536 | bytes 9175040
  300.3 4.3 copy.152
  304.6 6.5 reshape.430
  311.1 9.5 %all-to-all-start.2 = ((f32[32,1,8192]{2,1,0:T(1,128)}), f32[32,1,8192]{2,1,0:T(1,128)S(1)}, u32[]{:S(2)}, u32[]{:S(2)}) async-start(f32[32,1,8192]{2,1,0:T(1,128)} %reshape.430), calls=%async_computation.2 | async-start | bytes 2097152 | tf_op jit(solution)/shard_map/all_to_all | solution.py:143
  320.7 16.5 %fusion.21 = f32[32,4,128,128]{3,0,2,1:T(8,128)} fusion(f32[32,4,128,128]{3,2,1,0:T(8,128)} %bitcast.323, f32[32,32]{1,0:T(8,128)S(1)} %copy-done), kind=kOutput, calls=%fused_computation.38 | convolution fusion | flops 805306368 | bytes 16781312 | tf_op jit(solution)/shard_map/scpyz,co->sopyz/dot_general | solution.py:147
  340.6 4.9 reshape.431
  345.4 7.6 copy.154
  358.7 3.4 fusion.53
  363.3 41.2 %fusion.13 = f32[32,4,128,128]{3,2,1,0:T(8,128)S(1)} fusion(bf16[1,32,4,128,128]{4,3,2,1,0:T(8,128)(2,1)S(1)} %copy-done.2, f32[32,4,128,128]{3,0,2,1:T(8,128)S(1)} %bitcast.343, f32[32]{0:T(128)S(1)} %copy-done.3, f32[1,32,4,128,32]{3,4,2,1,0:T(8,128)S(1)} %get-tuple-element.23, f32[1,32,4,128,32]{3,4,2,1,0:T(8,128)S(1)} %get-tuple-element.22, ...), kind=kOutput, calls=%fused_computation.28 | convolution fusion | flops 1766858752 | bytes 25198720 | tf_op jit(solution)/shard_map/scpyj,zj->scpyz/dot_general | solution.py:72
  404.5 3.4 copy-done.1
  407.9 5.3 fusion.67
  413.3 3.6 fusion.49
  419.4 3.4 copy.246
  425.2 8.9 %fusion.107 = f32[1024,1,4,2,32]{4,3,2,1,0:T(2,128)} fusion(f32[1,32,4,1,1024]{1,3,2,0,4:T(1,128)} %bitcast.345, f32[1,32,4,1,1024]{1,3,2,0,4:T(1,128)} %bitcast.347), kind=kLoop, calls=%fused_computation.186 | loop fusion | flops 262144 | bytes 2097152
  434.1 5.8 reshape.432
  439.9 25.2 %all_to_all.65 = f32[32,1,8192]{2,1,0:T(1,128)S(1)} all-to-all(f32[32,1,8192]{2,1,0:T(1,128)S(1)} %reshape.432), channel_id=1, replica_groups=mesh['dp'=4,'mp'=32] {'mp'}, dimensions={0} | all-to-all | bytes 2097152 | tf_op jit(solution)/shard_map/all_to_all | solution.py:152
  468.3 4.9 reshape.433
  473.2 7.5 copy.247
  480.7 6.6 copy.163
  487.3 3.8 copy.164
  493.2 5.8 add_bitcast_fusion
  499.0 14.1 %pad_maximum_fusion = f32[2,32,32,32,32]{4,3,2,1,0:T(8,128)} fusion(f32[1,32,32,32,32]{4,3,2,1,0:T(8,128)S(1)} %get-tuple-element.29, f32[1,32,32,32,32]{4,3,2,1,0:T(8,128)S(1)} %get-tuple-element.28), kind=kLoop, calls=%fused_computation | loop fusion | flops 2097152 | bytes 16777216 | tf_op jit(solution)/shard_map/stack | solution.py:114
  513.1 15.8 %fusion.1 = (f32[32,32,32]{1,0,2:T(8,128)S(1)}, f32[32,32,32]{1,0,2:T(8,128)S(1)}, f32[32,32,32]{1,0,2:T(8,128)S(1)}, f32[32,32,32]{1,0,2:T(8,128)S(1)}) fusion(f32[2,32,32,4,8,32]{5,4,3,2,1,0:T(8,128)} %bitcast.322, f32[32,32,32]{1,0,2:T(8,128)S(1)} %copy.254, f32[32,32,32]{1,0,2:T(8,128)S(1)} %copy.255), kind=kLoop, calls=%fused_computation.5 | loop fusion | flops 8257536 | bytes 9175040
  533.1 4.5 copy.167
  537.6 6.5 reshape.434
  544.2 5.2 all-to-all-start.4
  549.4 17.5 %fusion.18 = f32[4,128,128,32]{2,3,1,0:T(8,128)} fusion(f32[32,4,128,128]{3,2,1,0:T(8,128)} %copy-done.1, f32[32,32]{1,0:T(8,128)S(1)} %copy-done), kind=kOutput, calls=%fused_computation.34 | convolution fusion | flops 805306368 | bytes 16781312 | tf_op jit(solution)/shard_map/sopyz,co->scpyz/dot_general | solution.py:166
  570.1 4.9 reshape.435
  574.9 7.8 copy.169
  588.6 3.4 fusion.52
  592.5 22.5 %fusion.17 = f32[1,32,4,128,128]{4,3,2,1,0:T(8,128)} fusion(f32[4,128,128,32]{2,3,1,0:T(8,128)S(1)} %bitcast.325, f32[1,32,4,128,32]{3,4,2,1,0:T(8,128)S(1)} %get-tuple-element.17, f32[1,32,4,128,32]{3,4,2,1,0:T(8,128)S(1)} %get-tuple-element.16, f32[128,32]{0,1:T(8,128)S(1)} %get-tuple-element.48, f32[128,32]{0,1:T(8,128)S(1)} %get-tuple-element.49), kind=kOutput, calls=%fused_computation.33 | convolution fusion | flops 1613766656 | bytes 21004288 | tf_op jit(solution)/shard_map/scpyj,zj->scpyz/dot_general | solution.py:72
  615.0 189.8 %reduce-scatter.2.cloned.1.call-done = f32[2,32,32,8,32]{4,3,2,1,0:T(8,128)} async-done(((f32[2,32,32,32,32]{4,3,2,1,0:T(8,128)}), f32[2,32,32,8,32]{4,3,2,1,0:T(8,128)}) %reduce-scatter.2.cloned.1.call-update) | async-done | bytes 2097168 | tf_op jit(solution)/shard_map/reduce_scatter | solution.py:158
  (74 shorter events, 52.4 us)
Async XLA Ops:
  7.2 313.5 %copy-start = (f32[32,32]{1,0:T(8,128)S(1)}, f32[32,32]{1,0:T(8,128)}, u32[]{:S(2)}) copy-start(f32[32,32]{1,0:T(8,128)} %param.8) | copy-start | bytes 12292
  41.6 58.6 %all-to-all-start = ((f32[32,1,8192]{2,1,0:T(1,128)}), f32[32,1,8192]{2,1,0:T(1,128)S(1)}, u32[]{:S(2)}, u32[]{:S(2)}) async-start(f32[32,1,8192]{2,1,0:T(1,128)} %reshape.428), calls=%async_computation | async-start | bytes 2097152 | tf_op jit(solution)/shard_map/all_to_all | solution.py:133
  100.2 99.4 %all-to-all-start.1 = ((f32[4,1,524288]{2,1,0:T(1,128)}), f32[4,1,524288]{2,1,0:T(1,128)}, u32[]{:S(2)}, u32[]{:S(2)}) async-start(f32[4,1,524288]{2,1,0:T(1,128)} %reshape.426), calls=%async_computation.1 | async-start | bytes 16777216 | tf_op jit(solution)/shard_map/all_to_all | solution.py:138
  311.1 26.3 %all-to-all-start.2 = ((f32[32,1,8192]{2,1,0:T(1,128)}), f32[32,1,8192]{2,1,0:T(1,128)S(1)}, u32[]{:S(2)}, u32[]{:S(2)}) async-start(f32[32,1,8192]{2,1,0:T(1,128)} %reshape.430), calls=%async_computation.2 | async-start | bytes 2097152 | tf_op jit(solution)/shard_map/all_to_all | solution.py:143
  320.7 484.2 %reduce-scatter.2.cloned.1.call-start = ((), (), s32[]{:S(2)}) async-start(), calls=%async_computation.6 | async-start | bytes 41943040 | tf_op jit(solution)/shard_map/reduce_scatter | solution.py:158
  358.7 4.2 slice-start.2
  358.7 4.2 slice-start.3
  358.7 4.6 copy-start.2
  358.7 4.6 copy-start.3
  404.5 3.4 copy-start.1
  544.2 22.7 %all-to-all-start.4 = ((f32[32,1,8192]{2,1,0:T(1,128)}), f32[32,1,8192]{2,1,0:T(1,128)S(1)}, u32[]{:S(2)}, u32[]{:S(2)}) async-start(f32[32,1,8192]{2,1,0:T(1,128)} %reshape.434), calls=%async_computation.4 | async-start | bytes 2097152 | tf_op jit(solution)/shard_map/all_to_all | solution.py:162
  588.6 3.9 slice-start
  588.6 3.9 slice-start.1
Sparse Core Ops, SparseCore 0:
  513.2 291.5 reduce-scatter.1
